TPU v7x, 256 devices: a whole 4x4x8 slice. The times are simulated.
256 devices in a mesh: zonal: 64 (over y_lo, x, z), merid: 4 (over y_hi, core).
Axes of the slice: x: 4, y: 4 (y_hi: 2, y_lo: 2; y = y_hi * 2 + y_lo), z: 8, core: 2. Of those that a mesh axis runs over, the one named last changes fastest.
Arguments:
- field: bfloat16 [64, 4096, 256], P('merid', 'zonal'), may hold values from -6 to 6
- weight_one: bfloat16 [3, 3, 256, 256], replicated, may hold values from -0.125 to 0.125
- bias_one: float32 [256], replicated, may hold values from -3 to 3
- weight_two: bfloat16 [3, 3, 256, 256], replicated, may hold values from -0.125 to 0.125
- bias_two: float32 [256], replicated, may hold values from -3 to 3
- depth_levels: int32 [64, 4096], P('merid', 'zonal'), may hold values from 0 to 64
- fold_partner: int32 [4096], replicated, may hold values from 0 to 4095, as said below
- cotangent: bfloat16 [64, 4096, 256], P('merid', 'zonal'), may hold values from -6 to 6
Outputs:
- output: bfloat16 [64, 4096, 256], P('merid', 'zonal')
- input_grad: bfloat16 [64, 4096, 256], P('merid', 'zonal')
- grad_one: float32 [3, 3, 256, 256], replicated
- grad_two: float32 [3, 3, 256, 256], replicated
Inputs may be any that keep to these rules, and one draw needn't show every extreme that they name: fold_partner[i] = (4095 - i + s) mod 4096 with one pivot offset s, 0 to 4095, for the whole table.
All inputs are finite; a program needn't handle non-finite values.
Results may differ from a plain program's by a relative error of at most 0.003.
Values may be sent and summed in bfloat16 or wider, within the bound.
No kernel may reach another device: no remote copies, remote signals or barrier semaphores. Data moves between devices by JAX's collectives and lax.ppermute only.
A program may use at most 128 MiB of HBM per device.

v0:
```python
import math
import jax
import jax.numpy as jnp
from jax import lax
from jax.sharding import PartitionSpec as P

LEV = 64


def with_halo(cells, sides, width, closed):
    for axis, dim in sides:
        count = lax.axis_size(axis)
        ends = count if closed else count - 1
        head = lax.slice_in_dim(cells, 0, width, axis=dim)
        tail = lax.slice_in_dim(cells, cells.shape[dim] - width, cells.shape[dim], axis=dim)
        cells = jnp.concatenate(
            [
                lax.ppermute(tail, axis, [(i, (i + 1) % count) for i in range(ends)]),
                cells,
                lax.ppermute(head, axis, [((i + 1) % count, i) for i in range(ends)]),
            ],
            axis=dim,
        )
    return cells


def level_mask(depth_levels, channels):
    level_index = lax.broadcasted_iota(jnp.int32, (1, 1, channels), 2) % LEV
    return (level_index < depth_levels[:, :, None]).astype(jnp.float32)


def fold_forward(top_row, fold_partner):
    columns = top_row.shape[0]
    whole_row = lax.all_gather(top_row, "zonal", axis=0, tiled=True)
    partners = lax.dynamic_slice_in_dim(fold_partner, lax.axis_index("zonal") * columns, columns, 0)
    return jnp.take(whole_row, partners, axis=0)


def fold_backward(fold_grad, fold_partner):
    columns = fold_grad.shape[0]
    whole_row = lax.all_gather(fold_grad.astype(jnp.bfloat16), "zonal", axis=0, tiled=True).astype(
        fold_grad.dtype
    )
    partners = lax.dynamic_slice_in_dim(fold_partner, lax.axis_index("zonal") * columns, columns, 0)
    return jnp.take(whole_row, partners, axis=0)


def pad_field(values, fold_partner, is_top):
    with_rows = with_halo(values, (("merid", 0),), 1, False)
    fold_row = fold_forward(values[-1], fold_partner)
    upper_row = jnp.where(is_top, fold_row, with_rows[-1])
    with_rows = jnp.concatenate([with_rows[:-1], upper_row[None]], axis=0)
    return with_halo(with_rows, (("zonal", 1),), 1, True)


def unpad_grad(grad_pad, fold_partner, is_top):
    sides = jnp.concatenate([grad_pad[:, :1], grad_pad[:, -1:]], axis=1)
    returned = with_halo(sides.astype(jnp.bfloat16), (("zonal", 1),), 1, True).astype(sides.dtype)
    inner = grad_pad[:, 1:-1]
    inner = inner.at[:, 0].add(returned[:, 0]).at[:, -1].add(returned[:, 3])
    rims = jnp.concatenate([inner[:1], inner[-1:]], axis=0)
    back_rows = with_halo(rims.astype(jnp.bfloat16), (("merid", 0),), 1, False).astype(rims.dtype)
    folded = fold_backward(inner[-1], fold_partner)
    top_added = back_rows[3] + jnp.where(is_top, folded, jnp.zeros_like(folded))
    middle = inner[1:-1]
    return middle.at[0].add(back_rows[0]).at[-1].add(top_added)


def patches_of(padded, rows, columns):
    pieces = [
        padded[row_step : row_step + rows, col_step : col_step + columns]
        for row_step in range(3)
        for col_step in range(3)
    ]
    return jnp.concatenate(pieces, axis=2).reshape(rows * columns, -1)


def transpose_conv(delta, flat_weight, rows, columns):
    channels = delta.shape[1]
    parts = lax.dot_general(
        delta, flat_weight, (((1,), (1,)), ((), ())), preferred_element_type=jnp.float32
    )
    parts = parts.reshape(rows, columns, 9, channels)
    grad_pad = jnp.zeros((rows + 2, columns + 2, channels), jnp.float32)
    for row_step in range(3):
        for col_step in range(3):
            grad_pad = grad_pad.at[row_step : row_step + rows, col_step : col_step + columns].add(
                parts[:, :, 3 * row_step + col_step]
            )
    return grad_pad


def kernel_grad(patches, delta):
    channels = delta.shape[1]
    summed = lax.dot_general(
        patches, delta, (((0,), (0,)), ((), ())), preferred_element_type=jnp.float32
    )
    return summed.reshape(3, 3, channels, channels)


def shards(
    field, weight_one, bias_one, weight_two, bias_two, depth_levels, fold_partner, cotangent
):
    rows, columns, channels = field.shape
    is_top = lax.axis_index("merid") == lax.axis_size("merid") - 1
    mask = level_mask(depth_levels, channels)
    flat_one = weight_one.reshape(9 * channels, channels)
    flat_two = weight_two.reshape(9 * channels, channels)
    patches_one = patches_of(pad_field(field, fold_partner, is_top), rows, columns)
    pre_one = (
        jnp.dot(patches_one, flat_one, preferred_element_type=jnp.float32).reshape(
            rows, columns, channels
        )
        + bias_one
    )
    hidden = (jax.nn.gelu(pre_one) * mask).astype(jnp.bfloat16)
    patches_two = patches_of(pad_field(hidden, fold_partner, is_top), rows, columns)
    pre_two = jnp.dot(patches_two, flat_two, preferred_element_type=jnp.float32).reshape(
        rows, columns, channels
    )
    output = ((field.astype(jnp.float32) + pre_two + bias_two) * mask).astype(jnp.bfloat16)
    masked_grad = cotangent.astype(jnp.float32) * mask
    delta_two = masked_grad.astype(jnp.bfloat16).reshape(rows * columns, channels)
    grad_two = kernel_grad(patches_two, delta_two)
    hidden_grad = unpad_grad(
        transpose_conv(delta_two, flat_two, rows, columns), fold_partner, is_top
    )
    _, gelu_back = jax.vjp(jax.nn.gelu, pre_one)
    delta_one = (
        gelu_back(hidden_grad * mask)[0].astype(jnp.bfloat16).reshape(rows * columns, channels)
    )
    grad_one = kernel_grad(patches_one, delta_one)
    field_grad = unpad_grad(
        transpose_conv(delta_one, flat_one, rows, columns), fold_partner, is_top
    )
    input_grad = (masked_grad + field_grad).astype(jnp.bfloat16)
    grad_one, grad_two = lax.psum((grad_one, grad_two), ("zonal", "merid"))
    scale = 1.0 / math.sqrt(rows * columns * lax.axis_size("zonal") * lax.axis_size("merid"))
    return (output, input_grad, grad_one * scale, grad_two * scale)


def solution(mesh):
    placed = (
        P("merid", "zonal", None),
        P(),
        P(),
        P(),
        P(),
        P("merid", "zonal"),
        P(),
        P("merid", "zonal", None),
    )
    return jax.shard_map(
        shards,
        mesh=mesh,
        in_specs=placed,
        out_specs=(P("merid", "zonal", None), P("merid", "zonal", None), P(), P()),
        check_vma=False,
    )
```

profile of v0, /device:TPU:97, one launch (start us, length us, event | category | flops | bytes accessed | tf_op | source)
XLA Modules:
  0.0 1509.0 jit_solution(12286972379343277605)
XLA Ops:
  10.1 2.9 fusion.35
  14.0 2.7 copy-done.2
  16.6 2.4 fusion.27
  19.0 6.4 scatter-add.89
  26.8 4.3 add_select_fusion.1
  31.1 6.4 scatter-add.90
  39.0 2.4 fusion.24
  41.3 5.1 scatter-add.94
  46.5 2.4 fusion.23
  48.8 5.1 scatter-add.95
  55.4 2.4 fusion.20
  57.8 5.1 scatter-add.99
  62.9 2.4 fusion.19
  65.3 5.1 scatter-add.100
  70.5 2.9 collective-permute-start.8
  74.6 2.7 collective-permute-done.9
  83.2 6.8 collective-permute-start
  94.1 5.1 collective-permute-start.10
  101.2 157.8 %all-gather.9.cloned.1.call-done = bf16[1,4096,256]{2,1,0:T(8,128)(2,1)} async-done(((bf16[1,64,256]{2,1,0:T(8,128)(2,1)}), bf16[1,4096,256]{2,1,0:T(8,128)(2,1)}) %all-gather.9.cloned.1.call-update) | async-done | bytes 2097168 | tf_op jit(solution)/shard_map/all_gather | solution.py:34
  259.0 2.5 gather_fusion
  262.9 3.3 collective-permute-start.3
  276.2 282.4 %all-gather.13.cloned.1.call-done = bf16[1,4096,256]{2,1,0:T(8,128)(2,1)} async-done(((bf16[1,64,256]{2,1,0:T(8,128)(2,1)}), bf16[1,4096,256]{2,1,0:T(8,128)(2,1)}) %all-gather.13.cloned.1.call-update) | async-done | bytes 2097168 | tf_op jit(solution)/shard_map/all_gather | solution.py:41
  558.5 3.9 bitcast_convert_fusion.1
  562.4 2.8 gather_fusion.2
  565.4 5.2 fusion.8
  571.3 2.5 fusion.33
  574.0 3.4 copy-done.3
  579.7 6.4 scatter-add.110
  586.1 3.3 add_select_fusion
  589.4 3.3 scatter-add.111
  610.6 3.1 collective-permute-start.13
  619.2 50.8 %collective-permute-start.5 = (bf16[1,64,256]{2,1,0:T(8,128)(2,1)}, bf16[1,64,256]{2,1,0:T(8,128)(2,1)S(1)}, u32[]{:S(2)}, u32[]{:S(2)}) collective-permute-start(bf16[1,64,256]{2,1,0:T(8,128)(2,1)} %get-tuple-element.341), channel_id=1, source_target_pairs={{1,0},{2,1},{3,2},{5,4},{6,5},{7,6},{9,8},{10,9},{11,10},{13,12},{... | collective-permute-start | bytes 98312 | tf_op jit(solution)/shard_map/ppermute | solution.py:20
  670.0 4.3 collective-permute-start.4
  674.3 6.8 copy.30
  681.1 187.6 %all-gather.11.cloned.1.call-done = bf16[1,4096,256]{2,1,0:T(8,128)(2,1)} async-done(((bf16[1,64,256]{2,1,0:T(8,128)(2,1)}), bf16[1,4096,256]{2,1,0:T(8,128)(2,1)}) %all-gather.11.cloned.1.call-update) | async-done | bytes 2097168 | tf_op jit(solution)/shard_map/all_gather | solution.py:34
  868.7 2.6 gather_fusion.1
  873.5 2.5 collective-permute-start.7
  876.0 5.1 fusion.55
  884.6 6.8 copy.31
  891.4 5.1 fusion.56
  897.3 52.6 %collective-permute-start.14 = (bf16[1,64,256]{2,1,0:T(8,128)(2,1)S(1)}, bf16[1,64,256]{2,1,0:T(8,128)(2,1)S(1)}, u32[]{:S(2)}, u32[]{:S(2)}) collective-permute-start(bf16[1,64,256]{2,1,0:T(8,128)(2,1)S(1)} %copy-done.14), channel_id=1, source_target_pairs={{0,1},{1,2},{2,3},{4,5},{5,6},{6,7},{8,9},{9,10},{10,11},{12,13},{... | collective-permute-start | bytes 98312 | tf_op jit(solution)/shard_map/ppermute | solution.py:18
  951.9 4.7 collective-permute-done.15
  956.7 211.5 %all-gather.15.cloned.1.call-done = bf16[1,4096,256]{2,1,0:T(8,128)(2,1)} async-done(((bf16[1,64,256]{2,1,0:T(8,128)(2,1)}), bf16[1,4096,256]{2,1,0:T(8,128)(2,1)}) %all-gather.15.cloned.1.call-update) | async-done | bytes 2097168 | tf_op jit(solution)/shard_map/all_gather | solution.py:41
  1168.2 3.9 bitcast_convert_fusion
  1172.0 3.0 gather_fusion.3
  1176.3 4.5 fusion.1
  1180.8 316.5 %all-reduce.5.cloned.1.call-done = (f32[3,3,256,256]{3,2,1,0:T(8,128)}, f32[3,3,256,256]{3,2,1,0:T(8,128)}) async-done(((f32[3,3,256,256]{3,2,1,0:T(8,128)}, f32[3,3,256,256]{3,2,1,0:T(8,128)}), (f32[3,3,256,256]{3,2,1,0:T(8,128)}, f32[3,3,256,256]{3,2,1,0:T(8,128)})) %all-reduce.5.cloned.1.call-update) | async-done | bytes 4718608 | tf_op jit(solution)/shard_map/psum | solution.py:137
  1497.3 5.1 broadcast_multiply_fusion
  (164 shorter events, 68.6 us)
Async XLA Ops:
  7.2 558.2 %copy-start = (bf16[3,3,256,256]{3,2,1,0:T(8,128)(2,1)S(1)}, bf16[3,3,256,256]{3,2,1,0:T(8,128)(2,1)}, u32[]{:S(2)}) copy-start(bf16[3,3,256,256]{3,2,1,0:T(8,128)(2,1)} %param.65) | copy-start | bytes 3538948
  7.2 251.8 %all-gather.9.cloned.1.call-start = ((), (), s32[]{:S(2)}) async-start(), calls=%async_computation | async-start | bytes 2129920 | tf_op jit(solution)/shard_map/all_gather | solution.py:34
  8.7 549.8 %all-gather.13.cloned.1.call-start = ((), (), s32[]{:S(2)}) async-start(), calls=%async_computation.2 | async-start | bytes 2129920 | tf_op jit(solution)/shard_map/all_gather | solution.py:41
  8.8 556.6 %copy-start.25 = (s32[256]{0:T(256)}, s32[256]{0:T(256)S(1)}, u32[]{:S(2)}) copy-start(s32[256]{0:T(256)S(1)} %and_select_fusion) | copy-start | bytes 3076
  10.1 2.9 copy-start.8
  13.0 3.7 copy-start.2
  16.6 9.5 copy-start.27
  70.4 12.8 copy-start.17
  70.5 4.1 collective-permute-start.8
  73.4 188.2 %copy-start.4 = (bf16[16,64,256]{2,1,0:T(8,128)(2,1)S(1)}, bf16[16,64,256]{2,1,0:T(8,128)(2,1)}, u32[]{:S(2)}) copy-start(bf16[16,64,256]{2,1,0:T(8,128)(2,1)} %param.64) | copy-start | bytes 1572868
  73.4 3.8 collective-permute-start.9
  83.2 183.1 %copy-start.13 = (bf16[1,64,256]{2,1,0:T(8,128)(2,1)S(1)}, bf16[1,64,256]{2,1,0:T(8,128)(2,1)}, u32[]{:S(2)}) copy-start(bf16[1,64,256]{2,1,0:T(8,128)(2,1)} %get-tuple-element.324) | copy-start | bytes 98308
  83.2 785.5 %all-gather.11.cloned.1.call-start = ((), (), s32[]{:S(2)}) async-start(), calls=%async_computation.1 | async-start | bytes 2129920 | tf_op jit(solution)/shard_map/all_gather | solution.py:34
  83.2 178.4 %collective-permute-start = (bf16[1,64,256]{2,1,0:T(8,128)(2,1)S(1)}, bf16[1,64,256]{2,1,0:T(8,128)(2,1)S(1)}, u32[]{:S(2)}, u32[]{:S(2)}) collective-permute-start(bf16[1,64,256]{2,1,0:T(8,128)(2,1)S(1)} %copy-done.17), channel_id=1, source_target_pairs={{0,1},{1,2},{2,3},{4,5},{5,6},{6,7},{8,9},{9,10},{10,11},{12,13},{... | collective-permute-start | bytes 98312 | tf_op jit(solution)/shard_map/ppermute | solution.py:18
  90.1 171.5 %collective-permute-start.1 = (bf16[1,64,256]{2,1,0:T(8,128)(2,1)S(1)}, bf16[1,64,256]{2,1,0:T(8,128)(2,1)S(1)}, u32[]{:S(2)}, u32[]{:S(2)}) collective-permute-start(bf16[1,64,256]{2,1,0:T(8,128)(2,1)S(1)} %get-tuple-element.343), channel_id=1, source_target_pairs={{1,0},{2,1},{3,2},{5,4},{6,5},{7,6},{9,8},{10,9},{11,10},{13,12},{... | collective-permute-start | bytes 98312 | tf_op jit(solution)/shard_map/ppermute | solution.py:20
  92.8 472.5 %copy-start.22 = (pred[64]{0:T(512)(128)(4,1)}, pred[64]{0:T(512)(128)(4,1)S(1)}, u32[]{:S(2)}) copy-start(pred[64]{0:T(512)(128)(4,1)S(1)} %get-tuple-element.320) | copy-start | bytes 196
  92.8 469.7 %copy-start.24 = (s32[1024]{0:T(1024)}, s32[1024]{0:T(1024)S(1)}, u32[]{:S(2)}) copy-start(s32[1024]{0:T(1024)S(1)} %pad_clamp_fusion) | copy-start | bytes 12292
  94.1 172.1 %collective-permute-start.10 = (bf16[1,64,256]{2,1,0:T(8,128)(2,1)}, bf16[1,64,256]{2,1,0:T(8,128)(2,1)S(1)}, u32[]{:S(2)}, u32[]{:S(2)}) collective-permute-start(bf16[1,64,256]{2,1,0:T(8,128)(2,1)} %get-tuple-element.324), channel_id=1, source_target_pairs={{0,1},{1,2},{2,3},{4,5},{5,6},{6,7},{8,9},{9,10},{10,11},{12,13},{... | collective-permute-start | bytes 98312 | tf_op jit(solution)/shard_map/ppermute | solution.py:18
  99.3 167.0 %collective-permute-start.11 = (bf16[1,64,256]{2,1,0:T(8,128)(2,1)S(1)}, bf16[1,64,256]{2,1,0:T(8,128)(2,1)S(1)}, u32[]{:S(2)}, u32[]{:S(2)}) collective-permute-start(bf16[1,64,256]{2,1,0:T(8,128)(2,1)S(1)} %get-tuple-element.325), channel_id=1, source_target_pairs={{1,0},{2,1},{3,2},{5,4},{6,5},{7,6},{9,8},{10,9},{11,10},{13,12},{... | collective-permute-start | bytes 98312 | tf_op jit(solution)/shard_map/ppermute | solution.py:20
  261.7 5.7 collective-permute-start.2
  262.9 4.4 collective-permute-start.3
  276.2 289.3 %copy-start.20 = (s32[16,64]{1,0:T(8,128)S(1)}, s32[16,64]{1,0:T(8,128)}, u32[]{:S(2)}) copy-start(s32[16,64]{1,0:T(8,128)} %param.69) | copy-start | bytes 12292
  276.2 289.3 %copy-start.28 = (f32[256]{0:T(256)S(1)}, f32[256]{0:T(256)}, u32[]{:S(2)}) copy-start(f32[256]{0:T(256)} %param.66) | copy-start | bytes 3076
  571.2 596.9 %all-gather.15.cloned.1.call-start = ((), (), s32[]{:S(2)}) async-start(), calls=%async_computation.3 | async-start | bytes 2129920 | tf_op jit(solution)/shard_map/all_gather | solution.py:41
  573.8 3.6 copy-start.3
  609.3 5.5 copy-start.15
  609.3 5.5 copy-start.16
  609.3 5.5 collective-permute-start.12
  610.6 4.2 collective-permute-start.13
  618.4 62.7 %copy-start.6 = (f32[18,64,256]{2,1,0:T(8,128)}, f32[18,64,256]{2,1,0:T(8,128)S(1)}, u32[]{:S(2)}) copy-start(f32[18,64,256]{2,1,0:T(8,128)S(1)} %scatter-add.125) | copy-start | bytes 3538948
  619.1 878.2 %all-reduce.5.cloned.1.call-start = ((), (), s32[]{:S(2)}) async-start(), calls=%async_computation.4 | async-start | bytes 9437184 | tf_op jit(solution)/shard_map/psum | solution.py:137
  619.2 252.2 %collective-permute-start.5 = (bf16[1,64,256]{2,1,0:T(8,128)(2,1)}, bf16[1,64,256]{2,1,0:T(8,128)(2,1)S(1)}, u32[]{:S(2)}, u32[]{:S(2)}) collective-permute-start(bf16[1,64,256]{2,1,0:T(8,128)(2,1)} %get-tuple-element.341), channel_id=1, source_target_pairs={{1,0},{2,1},{3,2},{5,4},{6,5},{7,6},{9,8},{10,9},{11,10},{13,12},{... | collective-permute-start | bytes 98312 | tf_op jit(solution)/shard_map/ppermute | solution.py:20
  670.0 201.4 %collective-permute-start.4 = (bf16[1,64,256]{2,1,0:T(8,128)(2,1)}, bf16[1,64,256]{2,1,0:T(8,128)(2,1)S(1)}, u32[]{:S(2)}, u32[]{:S(2)}) collective-permute-start(bf16[1,64,256]{2,1,0:T(8,128)(2,1)} %get-tuple-element.340), channel_id=1, source_target_pairs={{0,1},{1,2},{2,3},{4,5},{5,6},{6,7},{8,9},{9,10},{10,11},{12,13},{... | collective-permute-start | bytes 98312 | tf_op jit(solution)/shard_map/ppermute | solution.py:18
  674.3 197.0 %copy-start.23 = (pred[64]{0:T(512)(128)(4,1)S(1)}, pred[64]{0:T(512)(128)(4,1)}, u32[]{:S(2)}) copy-start(pred[64]{0:T(512)(128)(4,1)} %copy-done.22) | copy-start | bytes 196
  674.3 201.7 %copy-start.12 = (bf16[16,64,256]{2,1,0:T(8,128)(2,1)S(1)}, bf16[16,64,256]{2,1,0:T(8,128)(2,1)}, u32[]{:S(2)}) copy-start(bf16[16,64,256]{2,1,0:T(8,128)(2,1)} %get-tuple-element.326) | copy-start | bytes 1572868
  871.5 9.7 collective-permute-start.6
  873.5 7.7 collective-permute-start.7
  882.4 2.2 copy-start.5
  884.6 6.8 copy-start.9
  896.5 55.3 %copy-start.7 = (f32[18,64,256]{2,1,0:T(8,128)S(1)}, f32[18,64,256]{2,1,0:T(8,128)}, u32[]{:S(2)}) copy-start(f32[18,64,256]{2,1,0:T(8,128)} %copy-done.6) | copy-start | bytes 3538948
  897.3 54.6 %collective-permute-start.14 = (bf16[1,64,256]{2,1,0:T(8,128)(2,1)S(1)}, bf16[1,64,256]{2,1,0:T(8,128)(2,1)S(1)}, u32[]{:S(2)}, u32[]{:S(2)}) collective-permute-start(bf16[1,64,256]{2,1,0:T(8,128)(2,1)S(1)} %copy-done.14), channel_id=1, source_target_pairs={{0,1},{1,2},{2,3},{4,5},{5,6},{6,7},{8,9},{9,10},{10,11},{12,13},{... | collective-permute-start | bytes 98312 | tf_op jit(solution)/shard_map/ppermute | solution.py:18
  949.9 6.7 collective-permute-start.15
  956.6 218.5 %copy-start.10 = (bf16[16,64,256]{2,1,0:T(8,128)(2,1)S(1)}, bf16[16,64,256]{2,1,0:T(8,128)(2,1)}, u32[]{:S(2)}) copy-start(bf16[16,64,256]{2,1,0:T(8,128)(2,1)} %param.71) | copy-start | bytes 1572868
  956.6 218.5 %copy-start.21 = (s32[16,64]{1,0:T(8,128)S(1)}, s32[16,64]{1,0:T(8,128)}, u32[]{:S(2)}) copy-start(s32[16,64]{1,0:T(8,128)} %param.69) | copy-start | bytes 12292
  956.6 218.5 %copy-start.26 = (s32[256]{0:T(256)S(1)}, s32[256]{0:T(256)}, u32[]{:S(2)}) copy-start(s32[256]{0:T(256)} %copy-done.25) | copy-start | bytes 3076
  1172.0 4.2 copy-start.29
  1175.0 1.3 copy-start.11
  1497.3 5.1 copy-start.1
  (3 other events, 2.0 us)
Sparse Core Ops, SparseCore 0:
  10.4 248.6 all-gather.8
  261.4 297.1 all-gather.12
  571.4 297.2 all-gather.10
  870.3 297.7 all-gather.14
  1174.2 323.0 all-reduce.4
where the time goes:
time: 1510 us
  waiting for transfers between devices  1160 us (77%)
  starting transfers between devices  142 us (9%)
  local copies, waits for them, and re-layouts  106 us (7%)
  other arithmetic  56.4 us (4%)
  matrix products  25.3 us (2%)
    all_gather x2, waiting for transfers between devices, fold_backward(): lax.all_gather(fold_grad.astype(jnp.bfloat16), 'zonal', axis=0, tiled=True)  494 us
    all_gather x2, waiting for transfers between devices, fold_forward(): whole_row = lax.all_gather(top_row, 'zonal', axis=0, tiled=True)  345 us
    psum x1, waiting for transfers between devices, shards(): grad_one, grad_two = lax.psum((grad_one, grad_two), ('zonal', 'merid'))  317 us
    ppermute x8, starting transfers between devices, with_halo(): lax.ppermute(tail, axis, [(i, (i + 1) % count) for i in range(ends)])  76.3 us
    ppermute x8, starting transfers between devices, with_halo(): lax.ppermute(head, axis, [((i + 1) % count, i) for i in range(ends)])  65.5 us
    scatter-add x14, local copies, waits for them, and re-layouts, transpose_conv(): grad_pad.at[row_step:row_step + rows, col_step:col_step + columns]  51.2 us
  transfers between devices with their start and end apart: 21, of which 9 were waited for; matrix products, arithmetic and copies ran while one was open for 10% of the time, Pallas kernels for 0%

commit v1 on v0

--- a/solution.py
+++ b/solution.py
@@ -134,7 +134,7 @@
         transpose_conv(delta_one, flat_one, rows, columns), fold_partner, is_top
     )
     input_grad = (masked_grad + field_grad).astype(jnp.bfloat16)
-    grad_one, grad_two = lax.psum((grad_one, grad_two), ("zonal", "merid"))
+    grad_one, grad_two = lax.psum(lax.psum((grad_one, grad_two), "merid"), "zonal")
     scale = 1.0 / math.sqrt(rows * columns * lax.axis_size("zonal") * lax.axis_size("merid"))
     return (output, input_grad, grad_one * scale, grad_two * scale)
 

time: 1510 us -> 1990 us (1.32)
  the two profiles are of different devices: /device:TPU:97 before, /device:TPU:16 now
where the time goes in v1:
time: 1990 us
  waiting for transfers between devices  1700 us (85%)
  local copies, waits for them, and re-layouts  128 us (6%)
  other arithmetic  65.3 us (3%)
  starting transfers between devices  54.3 us (3%)
  matrix products  23.6 us (1%)
    psum x1, waiting for transfers between devices, shards(): lax.psum(lax.psum((grad_one, grad_two), 'merid'), 'zonal')  607 us
    all_gather x2, waiting for transfers between devices, fold_backward(): lax.all_gather(fold_grad.astype(jnp.bfloat16), 'zonal', axis=0, tiled=True)  574 us
    all_gather x2, waiting for transfers between devices, fold_forward(): whole_row = lax.all_gather(top_row, 'zonal', axis=0, tiled=True)  494 us
    scatter-add x14, local copies, waits for them, and re-layouts, transpose_conv(): grad_pad.at[row_step:row_step + rows, col_step:col_step + columns]  67.1 us
    ppermute x8, starting transfers between devices, with_halo(): lax.ppermute(head, axis, [((i + 1) % count, i) for i in range(ends)])  41.5 us
  transfers between devices with their start and end apart: 22, of which 10 were waited for; matrix products, arithmetic and copies ran while one was open for 9% of the time, Pallas kernels for 0%

profile of v1, /device:TPU:16, one launch (start us, length us, event | category | flops | bytes accessed | tf_op | source)
XLA Modules:
  0.0 1990.2 jit_solution(17625220805685448609)
XLA Ops:
  10.1 2.7 fusion.35
  13.8 2.7 copy-done.1
  16.5 2.4 fusion.27
  18.9 6.4 scatter-add.89
  26.7 4.3 add_select_fusion.1
  31.1 6.5 scatter-add.90
  41.4 5.1 scatter-add.94
  48.9 5.1 scatter-add.95
  57.8 5.1 scatter-add.99
  65.3 5.1 scatter-add.100
  72.6 6.9 collective-permute-start.9
  90.9 5.1 collective-permute-start.1
  100.1 5.1 collective-permute-start.11
  105.3 207.7 %all-gather.9.cloned.1.call-done = bf16[1,4096,256]{2,1,0:T(8,128)(2,1)} async-done(((bf16[1,64,256]{2,1,0:T(8,128)(2,1)}), bf16[1,4096,256]{2,1,0:T(8,128)(2,1)}) %all-gather.9.cloned.1.call-update) | async-done | bytes 2097168 | tf_op jit(solution)/shard_map/all_gather | solution.py:34
  312.9 2.5 gather_fusion
  316.2 5.7 collective-permute-start.3
  332.6 279.8 %all-gather.13.cloned.1.call-done = bf16[1,4096,256]{2,1,0:T(8,128)(2,1)} async-done(((bf16[1,64,256]{2,1,0:T(8,128)(2,1)}), bf16[1,4096,256]{2,1,0:T(8,128)(2,1)}) %all-gather.13.cloned.1.call-update) | async-done | bytes 2097168 | tf_op jit(solution)/shard_map/all_gather | solution.py:41
  612.4 3.9 bitcast_convert_fusion.1
  616.3 2.8 gather_fusion.2
  620.3 4.7 fusion.8
  627.6 2.4 collective-permute-start.4
  630.0 6.7 copy.30
  636.6 286.3 %all-gather.11.cloned.1.call-done = bf16[1,4096,256]{2,1,0:T(8,128)(2,1)} async-done(((bf16[1,64,256]{2,1,0:T(8,128)(2,1)}), bf16[1,4096,256]{2,1,0:T(8,128)(2,1)}) %all-gather.11.cloned.1.call-update) | async-done | bytes 2097168 | tf_op jit(solution)/shard_map/all_gather | solution.py:34
  922.9 2.5 gather_fusion.1
  926.3 5.6 collective-permute-start.7
  931.9 5.1 fusion.55
  940.5 6.7 copy.31
  947.2 5.1 fusion.56
  954.3 3.5 copy-done.2
  957.7 2.4 fusion.18
  960.2 6.4 scatter-add.110
  966.6 4.4 add_select_fusion
  971.0 6.5 scatter-add.111
  978.9 2.4 fusion.15
  981.3 5.1 scatter-add.115
  988.8 5.1 scatter-add.116
  997.8 5.1 scatter-add.120
  1005.3 5.1 scatter-add.121
  1010.7 6.2 collective-permute-start.13
  1024.8 26.6 %all-reduce.9.cloned.1.call-done = (f32[3,3,256,256]{3,2,1,0:T(8,128)}, f32[3,3,256,256]{3,2,1,0:T(8,128)}) async-done(((f32[3,3,256,256]{3,2,1,0:T(8,128)}, f32[3,3,256,256]{3,2,1,0:T(8,128)}), (f32[3,3,256,256]{3,2,1,0:T(8,128)}, f32[3,3,256,256]{3,2,1,0:T(8,128)})) %all-reduce.9.cloned.1.call-update) | async-done | bytes 4718608 | tf_op jit(solution)/shard_map/psum | solution.py:137
  1052.1 2.7 collective-permute-start.14
  1054.8 4.7 collective-permute-start.15
  1061.8 293.9 %all-gather.15.cloned.1.call-done = bf16[1,4096,256]{2,1,0:T(8,128)(2,1)} async-done(((bf16[1,64,256]{2,1,0:T(8,128)(2,1)}), bf16[1,4096,256]{2,1,0:T(8,128)(2,1)}) %all-gather.15.cloned.1.call-update) | async-done | bytes 2097168 | tf_op jit(solution)/shard_map/all_gather | solution.py:41
  1355.7 3.9 bitcast_convert_fusion
  1359.6 3.1 gather_fusion.3
  1366.5 4.5 fusion.1
  1371.1 607.3 %all-reduce.7.cloned.1.call-done = (f32[3,3,256,256]{3,2,1,0:T(8,128)}, f32[3,3,256,256]{3,2,1,0:T(8,128)}) async-done(((f32[3,3,256,256]{3,2,1,0:T(8,128)}, f32[3,3,256,256]{3,2,1,0:T(8,128)}), (f32[3,3,256,256]{3,2,1,0:T(8,128)}, f32[3,3,256,256]{3,2,1,0:T(8,128)})) %all-reduce.7.cloned.1.call-update) | async-done | bytes 4718608 | tf_op jit(solution)/shard_map/psum | solution.py:137
  1978.4 5.0 broadcast_multiply_fusion
  (163 shorter events, 81.1 us)
Async XLA Ops:
  7.2 613.1 %copy-start = (bf16[3,3,256,256]{3,2,1,0:T(8,128)(2,1)S(1)}, bf16[3,3,256,256]{3,2,1,0:T(8,128)(2,1)}, u32[]{:S(2)}) copy-start(bf16[3,3,256,256]{3,2,1,0:T(8,128)(2,1)} %param.65) | copy-start | bytes 3538948
  7.2 305.8 %all-gather.9.cloned.1.call-start = ((), (), s32[]{:S(2)}) async-start(), calls=%async_computation | async-start | bytes 2129920 | tf_op jit(solution)/shard_map/all_gather | solution.py:34
  8.7 603.7 %all-gather.13.cloned.1.call-start = ((), (), s32[]{:S(2)}) async-start(), calls=%async_computation.2 | async-start | bytes 2129920 | tf_op jit(solution)/shard_map/all_gather | solution.py:41
  8.8 4.0 copy-start.22
  12.8 3.7 copy-start.1
  16.4 9.5 copy-start.25
  70.6 10.6 copy-start.11
  70.6 10.6 copy-start.12
  70.6 10.6 collective-permute-start.8
  72.6 243.0 %copy-start.3 = (bf16[16,64,256]{2,1,0:T(8,128)(2,1)S(1)}, bf16[16,64,256]{2,1,0:T(8,128)(2,1)}, u32[]{:S(2)}) copy-start(bf16[16,64,256]{2,1,0:T(8,128)(2,1)} %param.64) | copy-start | bytes 1572868
  72.6 8.6 collective-permute-start.9
  88.9 233.0 %copy-start.9 = (bf16[1,64,256]{2,1,0:T(8,128)(2,1)S(1)}, bf16[1,64,256]{2,1,0:T(8,128)(2,1)}, u32[]{:S(2)}) copy-start(bf16[1,64,256]{2,1,0:T(8,128)(2,1)} %get-tuple-element.326) | copy-start | bytes 98308
  88.9 834.0 %all-gather.11.cloned.1.call-start = ((), (), s32[]{:S(2)}) async-start(), calls=%async_computation.1 | async-start | bytes 2129920 | tf_op jit(solution)/shard_map/all_gather | solution.py:34
  89.0 226.6 %collective-permute-start = (bf16[1,64,256]{2,1,0:T(8,128)(2,1)}, bf16[1,64,256]{2,1,0:T(8,128)(2,1)S(1)}, u32[]{:S(2)}, u32[]{:S(2)}) collective-permute-start(bf16[1,64,256]{2,1,0:T(8,128)(2,1)} %get-tuple-element.344), channel_id=1, source_target_pairs={{0,1},{1,2},{2,3},{4,5},{5,6},{6,7},{8,9},{9,10},{10,11},{12,13},{... | collective-permute-start | bytes 98312 | tf_op jit(solution)/shard_map/ppermute | solution.py:18
  90.9 224.6 %collective-permute-start.1 = (bf16[1,64,256]{2,1,0:T(8,128)(2,1)}, bf16[1,64,256]{2,1,0:T(8,128)(2,1)S(1)}, u32[]{:S(2)}, u32[]{:S(2)}) collective-permute-start(bf16[1,64,256]{2,1,0:T(8,128)(2,1)} %get-tuple-element.345), channel_id=1, source_target_pairs={{1,0},{2,1},{3,2},{5,4},{6,5},{7,6},{9,8},{10,9},{11,10},{13,12},{... | collective-permute-start | bytes 98312 | tf_op jit(solution)/shard_map/ppermute | solution.py:20
  96.8 828.6 %copy-start.19 = (pred[64]{0:T(512)(128)(4,1)}, pred[64]{0:T(512)(128)(4,1)S(1)}, u32[]{:S(2)}) copy-start(pred[64]{0:T(512)(128)(4,1)S(1)} %get-tuple-element.322) | copy-start | bytes 196
  96.9 826.1 %copy-start.21 = (s32[1024]{0:T(1024)}, s32[1024]{0:T(1024)S(1)}, u32[]{:S(2)}) copy-start(s32[1024]{0:T(1024)S(1)} %pad_clamp_fusion) | copy-start | bytes 12292
  98.2 223.8 %collective-permute-start.10 = (bf16[1,64,256]{2,1,0:T(8,128)(2,1)}, bf16[1,64,256]{2,1,0:T(8,128)(2,1)S(1)}, u32[]{:S(2)}, u32[]{:S(2)}) collective-permute-start(bf16[1,64,256]{2,1,0:T(8,128)(2,1)} %get-tuple-element.326), channel_id=1, source_target_pairs={{0,1},{1,2},{2,3},{4,5},{5,6},{6,7},{8,9},{9,10},{10,11},{12,13},{... | collective-permute-start | bytes 98312 | tf_op jit(solution)/shard_map/ppermute | solution.py:18
  100.1 221.8 %collective-permute-start.11 = (bf16[1,64,256]{2,1,0:T(8,128)(2,1)S(1)}, bf16[1,64,256]{2,1,0:T(8,128)(2,1)S(1)}, u32[]{:S(2)}, u32[]{:S(2)}) collective-permute-start(bf16[1,64,256]{2,1,0:T(8,128)(2,1)S(1)} %get-tuple-element.327), channel_id=1, source_target_pairs={{1,0},{2,1},{3,2},{5,4},{6,5},{7,6},{9,8},{10,9},{11,10},{13,12},{... | collective-permute-start | bytes 98312 | tf_op jit(solution)/shard_map/ppermute | solution.py:20
  315.6 8.1 collective-permute-start.2
  316.2 7.5 collective-permute-start.3
  332.6 287.6 %copy-start.17 = (s32[16,64]{1,0:T(8,128)S(1)}, s32[16,64]{1,0:T(8,128)}, u32[]{:S(2)}) copy-start(s32[16,64]{1,0:T(8,128)} %param.69) | copy-start | bytes 12292
  332.6 287.6 %copy-start.23 = (s32[256]{0:T(256)S(1)}, s32[256]{0:T(256)}, u32[]{:S(2)}) copy-start(s32[256]{0:T(256)} %copy-done.22) | copy-start | bytes 3076
  332.6 287.6 %copy-start.26 = (f32[256]{0:T(256)S(1)}, f32[256]{0:T(256)}, u32[]{:S(2)}) copy-start(f32[256]{0:T(256)} %param.66) | copy-start | bytes 3076
  619.3 1.0 copy-start.8
  625.6 425.7 %all-reduce.9.cloned.1.call-start = ((), (), s32[]{:S(2)}) async-start(), calls=%async_computation.5 | async-start | bytes 9437184 | tf_op jit(solution)/shard_map/psum | solution.py:137
  625.6 299.8 %collective-permute-start.5 = (bf16[1,64,256]{2,1,0:T(8,128)(2,1)S(1)}, bf16[1,64,256]{2,1,0:T(8,128)(2,1)S(1)}, u32[]{:S(2)}, u32[]{:S(2)}) collective-permute-start(bf16[1,64,256]{2,1,0:T(8,128)(2,1)S(1)} %get-tuple-element.343), channel_id=1, source_target_pairs={{1,0},{2,1},{3,2},{5,4},{6,5},{7,6},{9,8},{10,9},{11,10},{13,12},{... | collective-permute-start | bytes 98312 | tf_op jit(solution)/shard_map/ppermute | solution.py:20
  627.6 298.0 %collective-permute-start.4 = (bf16[1,64,256]{2,1,0:T(8,128)(2,1)}, bf16[1,64,256]{2,1,0:T(8,128)(2,1)S(1)}, u32[]{:S(2)}, u32[]{:S(2)}) collective-permute-start(bf16[1,64,256]{2,1,0:T(8,128)(2,1)} %get-tuple-element.342), channel_id=1, source_target_pairs={{0,1},{1,2},{2,3},{4,5},{5,6},{6,7},{8,9},{9,10},{10,11},{12,13},{... | collective-permute-start | bytes 98312 | tf_op jit(solution)/shard_map/ppermute | solution.py:18
  925.6 11.5 collective-permute-start.6
  926.3 10.8 collective-permute-start.7
  938.3 2.2 copy-start.4
  952.4 403.3 %all-gather.15.cloned.1.call-start = ((), (), s32[]{:S(2)}) async-start(), calls=%async_computation.3 | async-start | bytes 2129920 | tf_op jit(solution)/shard_map/all_gather | solution.py:41
  954.1 3.7 copy-start.2
  1010.6 8.2 collective-permute-start.12
  1010.7 8.1 collective-permute-start.13
  1024.7 953.6 %all-reduce.7.cloned.1.call-start = ((), (), s32[]{:S(2)}) async-start(), calls=%async_computation.4 | async-start | bytes 9437184 | tf_op jit(solution)/shard_map/psum | solution.py:137
  1051.3 0.8 copy-start.10
  1051.3 8.2 copy-start.5
  1052.1 8.6 collective-permute-start.14
  1054.8 6.3 collective-permute-start.15
  1060.7 295.0 %copy-start.13 = (bf16[1,64,256]{2,1,0:T(8,128)(2,1)}, bf16[1,64,256]{2,1,0:T(8,128)(2,1)S(1)}, u32[]{:S(2)}) copy-start(bf16[1,64,256]{2,1,0:T(8,128)(2,1)S(1)} %collective-permute-done.14) | copy-start | bytes 98308
  1061.1 294.5 %copy-start.14 = (bf16[1,64,256]{2,1,0:T(8,128)(2,1)}, bf16[1,64,256]{2,1,0:T(8,128)(2,1)S(1)}, u32[]{:S(2)}) copy-start(bf16[1,64,256]{2,1,0:T(8,128)(2,1)S(1)} %collective-permute-done.15) | copy-start | bytes 98308
  1061.8 300.9 %copy-start.20 = (pred[64]{0:T(512)(128)(4,1)S(1)}, pred[64]{0:T(512)(128)(4,1)}, u32[]{:S(2)}) copy-start(pred[64]{0:T(512)(128)(4,1)} %copy-done.19) | copy-start | bytes 196
  1061.8 302.5 %copy-start.6 = (bf16[16,64,256]{2,1,0:T(8,128)(2,1)S(1)}, bf16[16,64,256]{2,1,0:T(8,128)(2,1)}, u32[]{:S(2)}) copy-start(bf16[16,64,256]{2,1,0:T(8,128)(2,1)} %param.71) | copy-start | bytes 1572868
  1061.8 302.5 %copy-start.18 = (s32[16,64]{1,0:T(8,128)S(1)}, s32[16,64]{1,0:T(8,128)}, u32[]{:S(2)}) copy-start(s32[16,64]{1,0:T(8,128)} %param.69) | copy-start | bytes 12292
  1061.8 302.5 %copy-start.24 = (s32[256]{0:T(256)S(1)}, s32[256]{0:T(256)}, u32[]{:S(2)}) copy-start(s32[256]{0:T(256)} %copy-done.22) | copy-start | bytes 3076
  1359.6 6.9 copy-start.7
  1362.7 3.9 copy-start.27
  (2 other events, 1.2 us)
Sparse Core Ops, SparseCore 0:
  10.3 302.5 all-gather.8
  315.3 297.0 all-gather.12
  625.7 297.1 all-gather.10
  952.5 98.8 all-reduce.8
  1053.5 302.0 all-gather.14
  1358.2 620.0 all-reduce.6
